TPU v7x, 512 devices: a whole 4x4x16 slice. The times are simulated.
512 devices in a mesh: expert: 64 (over x, z), tensor: 8 (over y, core).
Axes of the slice: x: 4, y: 4, z: 16, core: 2. Of those that a mesh axis runs over, the one named last changes fastest.
Arguments:
- tokens: bfloat16 [1024, 7168], P('expert', 'tensor'), may hold values from -6 to 6
- expert_ids: int32 [1024, 8], P('expert'), may hold values from 0 to 31, as said below
- route_weights: float32 [1024, 8], P('expert'), may hold values from 0.05 to 1
- gate_weight: bfloat16 [64, 512, 7168], P('expert', 'tensor'), may hold values from -0.0625 to 0.0625
- up_weight: bfloat16 [64, 512, 7168], P('expert', 'tensor'), may hold values from -0.0625 to 0.0625
- down_weight: bfloat16 [64, 512, 7168], P('expert', 'tensor'), may hold values from -0.1875 to 0.1875
Outputs:
- mixed: bfloat16 [1024, 7168], P('expert', 'tensor')
Inputs may be any that keep to these rules, and one draw needn't show every extreme that they name: `expert_ids`: each row holds 8 different experts. One expert, the same for all tokens, is named by exactly 4 of the 16 tokens of every block of 16 consecutive tokens; every other expert by at most 4 tokens of a block.
All inputs are finite; a program needn't handle non-finite values.
Results may differ from a plain program's by a relative error of at most 0.015.
Values may be sent and summed in bfloat16 or wider, within the bound.
No kernel may reach another device: no remote copies, remote signals or barrier semaphores. Data moves between devices by JAX's collectives and lax.ppermute only.
A program may use at most 64 MiB of HBM per device.

v0:
```python
import jax
import jax.numpy as jnp
from jax import lax
from jax.sharding import PartitionSpec as P


def in_order(blocks, dim):
    shape = list(blocks.shape[1:])
    shape[dim] *= blocks.shape[0]
    return jnp.moveaxis(blocks, 0, dim).reshape(shape)


def sent_to_all(shard, axis):
    copies = jnp.broadcast_to(shard, (lax.axis_size(axis), *shard.shape))
    return lax.all_to_all(copies, axis, split_axis=0, concat_axis=0, tiled=True)


def gather_directly(shard, axis, dim):
    return in_order(sent_to_all(shard, axis), dim)


def rows_times(rows, weight):
    return lax.dot_general(
        rows, weight, (((1,), (1,)), ((), ())), preferred_element_type=jnp.float32
    )


def body(tokens, expert_ids, route_weights, gate_weight, up_weight, down_weight):
    devices_wide = lax.axis_size("expert")
    experts = devices_wide // 2
    tok_count = expert_ids.shape[0]
    per_token = expert_ids.shape[1]
    capacity = min(tok_count, tok_count * per_token // experts)
    slot_count = experts * capacity
    arrived_count = devices_wide * capacity
    expert_range = jnp.arange(experts, dtype=jnp.int32)
    onehot = jnp.sum(
        (expert_ids[:, :, None] == expert_range[None, None, :]).astype(jnp.int32), axis=1
    )
    earlier_count = jnp.cumsum(onehot, axis=0) - onehot
    slot_rank = jnp.take_along_axis(earlier_count, expert_ids, axis=1)
    slot_of = expert_ids * capacity + slot_rank
    slot_range = jnp.arange(slot_count, dtype=jnp.int32)
    select = jnp.any(slot_of[None, :, :] == slot_range[:, None, None], axis=2).astype(jnp.bfloat16)
    weight_gate = gate_weight[0]
    weight_up = up_weight[0]
    weight_out = down_weight[0]
    packed = jnp.dot(select, tokens, preferred_element_type=jnp.float32).astype(jnp.bfloat16)
    packed = packed.reshape(experts, capacity, tokens.shape[1])
    arrived = lax.all_to_all(
        jnp.repeat(packed, 2, axis=0), "expert", split_axis=0, concat_axis=0, tiled=True
    ).reshape(arrived_count, -1)
    shard_piece = lax.all_gather(arrived, "tensor", axis=1, tiled=True)
    gate_act = rows_times(shard_piece, weight_gate)
    up_act = rows_times(shard_piece, weight_up)
    hidden = (jax.nn.silu(gate_act) * up_act).astype(jnp.bfloat16)
    columns = lax.all_to_all(weight_out, "tensor", split_axis=1, concat_axis=0, tiled=True)
    unit_count = hidden.shape[1]
    shard_piece = gather_directly(hidden, "tensor", 1)
    groups = shard_piece.shape[1] // unit_count
    weight_rows = columns
    weight_rows = weight_rows.reshape(groups, unit_count, columns.shape[1])
    grouped = shard_piece.reshape(shard_piece.shape[0], groups, unit_count)
    group_terms = jnp.einsum(
        "rgf,gfd->grd", grouped, weight_rows, preferred_element_type=jnp.float32
    ).astype(jnp.bfloat16)
    group_terms = lax.optimization_barrier(group_terms)
    half_out = jnp.sum(group_terms.astype(jnp.float32), axis=0).astype(jnp.bfloat16)
    returned = lax.all_to_all(
        half_out.reshape(devices_wide, capacity, -1),
        "expert",
        split_axis=0,
        concat_axis=0,
        tiled=True,
    )
    returned = returned.reshape(experts, 2, capacity, -1).astype(jnp.float32)
    combined = (returned[:, 0] + returned[:, 1]).reshape(slot_count, -1)
    picked = combined[slot_of]
    mixed_out = jnp.sum(route_weights[:, :, None] * picked, axis=1)
    return mixed_out.astype(jnp.bfloat16)


def solution(mesh):
    placed = (
        P("expert", "tensor"),
        P("expert", None),
        P("expert", None),
        P("expert", "tensor", None),
        P("expert", "tensor", None),
        P("expert", "tensor", None),
    )
    return jax.shard_map(
        body, mesh=mesh, in_specs=placed, out_specs=P("expert", "tensor"), check_vma=False
    )
```

profile of v0, /device:TPU:6, one launch (start us, length us, event | category | flops | bytes accessed | tf_op | source)
XLA Modules:
  0.0 163.6 jit_solution(6472989712273088661)
XLA Ops:
  6.5 0.8 copy.21
  7.4 0.7 bitcast_or_fusion
  8.4 1.3 gather_fusion.1
  9.9 0.1 fusion.7
  10.1 0.3 convolution_convert_fusion.1
  10.4 0.1 broadcast_in_dim.19
  10.5 47.4 %all_to_all.31 = bf16[64,4,896]{2,1,0:T(4,128)(2,1)S(1)} all-to-all(bf16[64,4,896]{2,1,0:T(4,128)(2,1)S(1)} %bitcast.31), channel_id=1, replica_groups=mesh['expert'=64,'tensor'=8] {'expert'}, dimensions={0} | all-to-all | bytes 917504 | tf_op jit(solution)/shard_map/all_to_all | solution.py:50
  57.9 0.9 reshape.40
  58.8 0.1 copy.27
  59.0 1.1 copy.25
  60.0 4.6 %all-to-all-start.2 = ((bf16[64,8,896]{2,0,1:T(8,128)(2,1)}), bf16[64,8,896]{2,0,1:T(8,128)(2,1)S(1)}, u32[]{:S(2)}, u32[]{:S(2)}) async-start(bf16[64,8,896]{2,0,1:T(8,128)(2,1)} %copy.25), calls=%async_computation.2 | async-start | bytes 1835008 | tf_op jit(solution)/shard_map/all_to_all | solution.py:57
  64.7 30.6 %all-gather.2.cloned.1.call-done = bf16[256,7168]{1,0:T(8,128)(2,1)} async-done(((bf16[256,896]{1,0:T(8,128)(2,1)}), bf16[256,7168]{1,0:T(8,128)(2,1)}) %all-gather.2.cloned.1.call-update) | async-done | bytes 3670032 | tf_op jit(solution)/shard_map/all_gather | solution.py:53
  95.2 3.4 %fusion.3 = f32[256,64]{0,1:T(8,128)S(1)} fusion(bf16[256,7168]{1,0:T(8,128)(2,1)} %all-gather.2.cloned.1.call-done, bf16[1,64,7168]{2,1,0:T(8,128)(2,1)S(1)} %copy-done), kind=kOutput, calls=%fused_computation.8 | convolution fusion | flops 234881024 | bytes 4653056 | tf_op jit(solution)/shard_map/dot_general | solution.py:23
  98.7 1.2 fusion
  99.9 10.0 %all_to_all.32 = bf16[8,256,64]{1,2,0:T(8,128)(2,1)S(1)} all-to-all(bf16[8,256,64]{1,2,0:T(8,128)(2,1)S(1)} %broadcast_in_dim.20), channel_id=1, replica_groups=mesh['expert'=64,'tensor'=8] {'tensor'}, dimensions={0} | all-to-all | bytes 524288 | tf_op jit(solution)/shard_map/all_to_all | solution.py:15
  109.9 3.0 %convolution_convert_fusion = bf16[8,256,896]{2,1,0:T(8,128)(2,1)} fusion(bf16[64,8,896]{2,0,1:T(8,128)(2,1)S(1)} %all-to-all-done.2, bf16[8,256,64]{1,2,0:T(8,128)(2,1)S(1)} %all_to_all.32), kind=kOutput, calls=%fused_computation.2 | convolution fusion | flops 236716032 | bytes 4849664 | tf_op jit(solution)/shard_map/rgf,gfd->grd/dot_general | solution.py:64
  112.9 2.8 %reduce_sum.31 = bf16[256,896]{1,0:T(8,128)(2,1)S(1)} reduce(bf16[8,256,896]{2,1,0:T(8,128)(2,1)} %convolution_convert_fusion, bf16[]{:T(256)} %constant.31.clone.1), dimensions={0}, to_apply=%region_3.4 | reduce | flops 1605632 | bytes 4128770 | tf_op jit(solution)/shard_map/reduce_sum | solution.py:68
  115.6 0.9 reshape.41
  116.5 10.0 %all-to-all-start.3 = ((bf16[64,4,896]{2,1,0:T(4,128)(2,1)}), bf16[64,4,896]{2,1,0:T(4,128)(2,1)S(1)}, u32[]{:S(2)}, u32[]{:S(2)}) async-start(bf16[64,4,896]{2,1,0:T(4,128)(2,1)} %reshape.41), calls=%async_computation.3 | async-start | bytes 917504 | tf_op jit(solution)/shard_map/all_to_all | solution.py:69
  126.8 28.0 %all-to-all-done.3 = bf16[64,4,896]{2,1,0:T(4,128)(2,1)S(1)} async-done(((bf16[64,4,896]{2,1,0:T(4,128)(2,1)}), bf16[64,4,896]{2,1,0:T(4,128)(2,1)S(1)}, u32[]{:S(2)}, u32[]{:S(2)}) %all-to-all-start.3) | async-done | bytes 458784 | tf_op jit(solution)/shard_map/all_to_all | solution.py:69
  154.9 0.1 slice_add_fusion
  155.0 0.2 add.33
  155.2 0.8 gather_fusion
  156.0 0.8 fusion.5
  (33 shorter events, 1.0 us)
Async XLA Ops:
  6.5 88.7 %copy-start = (bf16[1,64,7168]{2,1,0:T(8,128)(2,1)S(1)}, bf16[1,64,7168]{2,1,0:T(8,128)(2,1)}, u32[]{:S(2)}) copy-start(bf16[1,64,7168]{2,1,0:T(8,128)(2,1)} %param.9) | copy-start | bytes 2752516
  6.5 88.7 %all-gather.2.cloned.1.call-start = ((), (), s32[]{:S(2)}) async-start(), calls=%async_computation.4 | async-start | bytes 4128768 | tf_op jit(solution)/shard_map/all_gather | solution.py:53
  8.4 1.5 copy-start.4
  8.4 1.7 %copy-start.5 = (bf16[16,896]{1,0:T(8,128)(2,1)S(1)}, bf16[16,896]{1,0:T(8,128)(2,1)}, u32[]{:S(2)}) copy-start(bf16[16,896]{1,0:T(8,128)(2,1)} %param.6) | copy-start | bytes 86020
  9.7 49.1 %copy-start.2 = (bf16[1,64,7168]{2,1,0:T(8,128)(2,1)S(1)}, bf16[1,64,7168]{2,1,0:T(8,128)(2,1)}, u32[]{:S(2)}) copy-start(bf16[1,64,7168]{2,1,0:T(8,128)(2,1)} %param.11) | copy-start | bytes 2752516
  60.0 38.6 %copy-start.3 = (bf16[1,64,7168]{2,1,0:T(8,128)(2,1)S(1)}, bf16[1,64,7168]{2,1,0:T(8,128)(2,1)}, u32[]{:S(2)}) copy-start(bf16[1,64,7168]{2,1,0:T(8,128)(2,1)} %param.10) | copy-start | bytes 2752516
  60.0 39.9 %all-to-all-start.2 = ((bf16[64,8,896]{2,0,1:T(8,128)(2,1)}), bf16[64,8,896]{2,0,1:T(8,128)(2,1)S(1)}, u32[]{:S(2)}, u32[]{:S(2)}) async-start(bf16[64,8,896]{2,0,1:T(8,128)(2,1)} %copy.25), calls=%async_computation.2 | async-start | bytes 1835008 | tf_op jit(solution)/shard_map/all_to_all | solution.py:57
  95.2 3.4 %copy-start.1 = (bf16[256,7168]{1,0:T(8,128)(2,1)S(1)}, bf16[256,7168]{1,0:T(8,128)(2,1)}, u32[]{:S(2)}) copy-start(bf16[256,7168]{1,0:T(8,128)(2,1)} %all-gather.2.cloned.1.call-done) | copy-start | bytes 11010052
  112.9 13.9 %copy-start.6 = (f32[16,8]{0,1:T(8,128)S(1)}, f32[16,8]{0,1:T(8,128)}, u32[]{:S(2)}) copy-start(f32[16,8]{0,1:T(8,128)} %param.8) | copy-start | bytes 1540
  116.5 38.3 %all-to-all-start.3 = ((bf16[64,4,896]{2,1,0:T(4,128)(2,1)}), bf16[64,4,896]{2,1,0:T(4,128)(2,1)S(1)}, u32[]{:S(2)}, u32[]{:S(2)}) async-start(bf16[64,4,896]{2,1,0:T(4,128)(2,1)} %reshape.41), calls=%async_computation.3 | async-start | bytes 917504 | tf_op jit(solution)/shard_map/all_to_all | solution.py:69
Sparse Core Ops, SparseCore 0:
  58.9 36.2 all-gather.1
where the time goes:
time: 164 us
  waiting for transfers between devices  58.6 us (36%)
  blocking collectives  57.4 us (35%)
  starting transfers between devices  14.6 us (9%)
  between operations  13.6 us (8%)
  matrix products  7.88 us (5%)
  local copies, waits for them, and re-layouts  6.9 us (4%)
  other arithmetic  4.69 us (3%)
    all_to_all x1, blocking collectives, body(): lax.all_to_all(jnp.repeat(packed, 2, axis=0), 'expert', split_axis=0, con...  47.4 us
    all_gather x1, waiting for transfers between devices, body(): shard_piece = lax.all_gather(arrived, 'tensor', axis=1, tiled=True)  30.6 us
    all_to_all x1, waiting for transfers between devices, body(): lax.all_to_all(half_out.reshape(devices_wide, capacity, -1), 'expert', sp...  28 us
    all_to_all x1, starting transfers between devices, body(): lax.all_to_all(half_out.reshape(devices_wide, capacity, -1), 'expert', sp...  10 us
    all_to_all x1, blocking collectives, sent_to_all(): return lax.all_to_all(copies, axis, split_axis=0, concat_axis=0, tiled=True)  9.98 us
    dot_general x2, matrix products, rows_times(): lax.dot_general(rows, weight, (((1,), (1,)), ((), ())), preferred_element...  4.66 us
    all_to_all x1, starting transfers between devices, body(): lax.all_to_all(weight_out, 'tensor', split_axis=1, concat_axis=0, tiled=T...  4.6 us
  transfers between devices with their start and end apart: 3, of which 2 were waited for; matrix products, arithmetic and copies ran while one was open for 4% of the time, Pallas kernels for 0%

commit v1 on v0

--- a/solution.py
+++ b/solution.py
@@ -50,7 +50,9 @@
     arrived = lax.all_to_all(
         jnp.repeat(packed, 2, axis=0), "expert", split_axis=0, concat_axis=0, tiled=True
     ).reshape(arrived_count, -1)
-    shard_piece = lax.all_gather(arrived, "tensor", axis=1, tiled=True)
+    shard_piece = jnp.concatenate(
+        lax.all_to_all(jnp.stack([arrived] * lax.axis_size("tensor")), "tensor", 0, 0), axis=1
+    )
     gate_act = rows_times(shard_piece, weight_gate)
     up_act = rows_times(shard_piece, weight_up)
     hidden = (jax.nn.silu(gate_act) * up_act).astype(jnp.bfloat16)

time: 164 us -> 175 us (1.067)
  waiting for transfers between devices: 58.6 us -> 79.8 us
  between operations: 13.6 us -> 0.21 us
    all_to_all x0 -> x1, waiting for transfers between devices: none -> 42.9 us  [body(): lax.all_to_all(jnp.stack([arrived] * lax.axis_size('tensor')), 'tensor',...]
    all_gather x1 -> x0, waiting for transfers between devices: 30.6 us -> none  [body(): shard_piece = lax.all_gather(arrived, 'tensor', axis=1, tiled=True)]
    all_to_all x1, waiting for transfers between devices: 0.01 us -> 8.92 us  [body(): lax.all_to_all(weight_out, 'tensor', split_axis=1, concat_axis=0, tiled=T...]
    all_to_all x0 -> x1, starting transfers between devices: none -> 4.63 us  [body(): lax.all_to_all(jnp.stack([arrived] * lax.axis_size('tensor')), 'tensor',...]
    all_to_all x1, starting transfers between devices: 10 us -> 6.97 us  [body(): lax.all_to_all(half_out.reshape(devices_wide, capacity, -1), 'expert', sp...]
    another operation x0 -> x3, local copies, waits for them, and re-layouts: none -> 2.39 us  [body(): jnp.stack([arrived] * lax.axis_size('tensor'))]
  transfers between devices with their start and end apart: 3 -> 3, of which waited for: 2 -> 3; matrix products, arithmetic and copies ran while one was open for 4% -> 4% of each run, Pallas kernels for 0% -> 0%
where the time goes in v1:
time: 175 us; the launch traced here: 174 us
  waiting for transfers between devices  79.8 us (46%)
  blocking collectives  57.3 us (33%)
  starting transfers between devices  15.2 us (9%)
  matrix products  8.73 us (5%)
  local copies, waits for them, and re-layouts  8.4 us (5%)
  other arithmetic  4.69 us (3%)
    all_to_all x1, blocking collectives, body(): lax.all_to_all(jnp.repeat(packed, 2, axis=0), 'expert', split_axis=0, con...  47.4 us
    all_to_all x1, waiting for transfers between devices, body(): lax.all_to_all(jnp.stack([arrived] * lax.axis_size('tensor')), 'tensor',...  42.9 us
    all_to_all x1, waiting for transfers between devices, body(): lax.all_to_all(half_out.reshape(devices_wide, capacity, -1), 'expert', sp...  28 us
    all_to_all x1, blocking collectives, sent_to_all(): return lax.all_to_all(copies, axis, split_axis=0, concat_axis=0, tiled=True)  9.91 us
    all_to_all x1, waiting for transfers between devices, body(): lax.all_to_all(weight_out, 'tensor', split_axis=1, concat_axis=0, tiled=T...  8.92 us
    all_to_all x1, starting transfers between devices, body(): lax.all_to_all(half_out.reshape(devices_wide, capacity, -1), 'expert', sp...  6.97 us
    dot_general x2, matrix products, rows_times(): lax.dot_general(rows, weight, (((1,), (1,)), ((), ())), preferred_element...  5.5 us
    all_to_all x1, starting transfers between devices, body(): lax.all_to_all(jnp.stack([arrived] * lax.axis_size('tensor')), 'tensor',...  4.63 us
  transfers between devices with their start and end apart: 3, of which 3 were waited for; matrix products, arithmetic and copies ran while one was open for 4% of the time, Pallas kernels for 0%

profile of v1, /device:TPU:6, one launch (start us, length us, event | category | flops | bytes accessed | tf_op | source)
XLA Modules:
  0.0 174.3 jit_solution(16874876397680388563)
XLA Ops:
  0.0 0.8 copy.30
  0.8 0.7 bitcast_or_fusion
  1.9 1.3 gather_fusion.1
  3.5 0.3 convolution_convert_fusion.1
  4.0 47.4 %all_to_all.36 = bf16[64,4,896]{2,1,0:T(4,128)(2,1)S(1)} all-to-all(bf16[64,4,896]{2,1,0:T(4,128)(2,1)S(1)} %bitcast.34), channel_id=1, replica_groups=mesh['expert'=64,'tensor'=8] {'expert'}, dimensions={0} | all-to-all | bytes 917504 | tf_op jit(solution)/shard_map/all_to_all | solution.py:50
  51.5 0.2 copy.34
  51.7 2.1 %stack.3 = bf16[8,256,896]{1,2,0:T(8,128)(2,1)} broadcast(bf16[256,896]{0,1:T(8,128)(2,1)S(1)} %copy.34), dimensions={1,2} | broadcast | bytes 4128768 | tf_op jit(solution)/shard_map/stack | solution.py:54
  53.8 4.6 %all-to-all-start.1 = ((bf16[8,256,896]{1,2,0:T(8,128)(2,1)}), bf16[8,256,896]{1,2,0:T(8,128)(2,1)}, u32[]{:S(2)}, u32[]{:S(2)}) async-start(bf16[8,256,896]{1,2,0:T(8,128)(2,1)} %stack.3), calls=%async_computation.1 | async-start | bytes 7340032 | tf_op jit(solution)/shard_map/all_to_all | solution.py:54
  58.4 0.1 copy.37
  58.6 1.1 copy.35
  59.6 42.9 %all-to-all-done.1 = bf16[8,256,896]{1,2,0:T(8,128)(2,1)} async-done(((bf16[8,256,896]{1,2,0:T(8,128)(2,1)}), bf16[8,256,896]{1,2,0:T(8,128)(2,1)}, u32[]{:S(2)}, u32[]{:S(2)}) %all-to-all-start.1) | async-done | bytes 3670048 | tf_op jit(solution)/shard_map/all_to_all | solution.py:54
  102.5 3.6 %all-to-all-start.3 = ((bf16[64,8,896]{2,0,1:T(8,128)(2,1)}), bf16[64,8,896]{2,0,1:T(8,128)(2,1)S(1)}, u32[]{:S(2)}, u32[]{:S(2)}) async-start(bf16[64,8,896]{2,0,1:T(8,128)(2,1)} %copy.35), calls=%async_computation.3 | async-start | bytes 1835008 | tf_op jit(solution)/shard_map/all_to_all | solution.py:59
  106.1 2.7 %fusion.3 = f32[256,64]{0,1:T(8,128)S(1)} fusion(bf16[256,7168]{0,1:T(8,128)(2,1)} %bitcast.3, bf16[1,64,7168]{2,1,0:T(8,128)(2,1)S(1)} %copy-done), kind=kOutput, calls=%fused_computation.8 | convolution fusion | flops 234881024 | bytes 4653056 | tf_op jit(solution)/shard_map/dot_general | solution.py:23
  108.8 2.8 %fusion = bf16[256,64]{0,1:T(8,128)(2,1)S(1)} fusion(bf16[256,7168]{0,1:T(8,128)(2,1)} %bitcast.3, bf16[1,64,7168]{2,1,0:T(8,128)(2,1)S(1)} %copy-done.2, f32[256,64]{0,1:T(8,128)S(1)} %fusion.3), kind=kOutput, calls=%fused_computation.5 | convolution fusion | flops 234979328 | bytes 4685824 | tf_op jit(solution)/shard_map/dot_general | solution.py:23
  111.6 8.9 %all-to-all-done.3 = bf16[64,8,896]{2,0,1:T(8,128)(2,1)S(1)} async-done(((bf16[64,8,896]{2,0,1:T(8,128)(2,1)}), bf16[64,8,896]{2,0,1:T(8,128)(2,1)S(1)}, u32[]{:S(2)}, u32[]{:S(2)}) %all-to-all-start.3) | async-done | bytes 917536 | tf_op jit(solution)/shard_map/all_to_all | solution.py:59
  120.5 9.9 %all_to_all.37 = bf16[8,256,64]{1,2,0:T(8,128)(2,1)S(1)} all-to-all(bf16[8,256,64]{1,2,0:T(8,128)(2,1)S(1)} %broadcast_in_dim.20), channel_id=1, replica_groups=mesh['expert'=64,'tensor'=8] {'tensor'}, dimensions={0} | all-to-all | bytes 524288 | tf_op jit(solution)/shard_map/all_to_all | solution.py:15
  130.4 3.0 %convolution_convert_fusion = bf16[8,256,896]{2,1,0:T(8,128)(2,1)} fusion(bf16[64,8,896]{2,0,1:T(8,128)(2,1)S(1)} %all-to-all-done.3, bf16[8,256,64]{1,2,0:T(8,128)(2,1)S(1)} %all_to_all.37), kind=kOutput, calls=%fused_computation.2 | convolution fusion | flops 236716032 | bytes 4849664 | tf_op jit(solution)/shard_map/rgf,gfd->grd/dot_general | solution.py:66
  133.4 2.8 %reduce_sum.31 = bf16[256,896]{1,0:T(8,128)(2,1)S(1)} reduce(bf16[8,256,896]{2,1,0:T(8,128)(2,1)} %convolution_convert_fusion, bf16[]{:T(256)} %constant.31.clone.1), dimensions={0}, to_apply=%region_3.4 | reduce | flops 1605632 | bytes 4128770 | tf_op jit(solution)/shard_map/reduce_sum | solution.py:70
  136.2 0.9 reshape.47
  137.0 7.0 %all-to-all-start.4 = ((bf16[64,4,896]{2,1,0:T(4,128)(2,1)}), bf16[64,4,896]{2,1,0:T(4,128)(2,1)S(1)}, u32[]{:S(2)}, u32[]{:S(2)}) async-start(bf16[64,4,896]{2,1,0:T(4,128)(2,1)} %reshape.47), calls=%async_computation.4 | async-start | bytes 917504 | tf_op jit(solution)/shard_map/all_to_all | solution.py:71
  144.3 28.0 %all-to-all-done.4 = bf16[64,4,896]{2,1,0:T(4,128)(2,1)S(1)} async-done(((bf16[64,4,896]{2,1,0:T(4,128)(2,1)}), bf16[64,4,896]{2,1,0:T(4,128)(2,1)S(1)}, u32[]{:S(2)}, u32[]{:S(2)}) %all-to-all-start.4) | async-done | bytes 458784 | tf_op jit(solution)/shard_map/all_to_all | solution.py:71
  172.5 0.2 add.33
  172.6 0.8 gather_fusion
  173.5 0.8 fusion.5
  (32 shorter events, 1.4 us)
Async XLA Ops:
  0.0 106.1 %copy-start = (bf16[1,64,7168]{2,1,0:T(8,128)(2,1)S(1)}, bf16[1,64,7168]{2,1,0:T(8,128)(2,1)}, u32[]{:S(2)}) copy-start(bf16[1,64,7168]{2,1,0:T(8,128)(2,1)} %param.9) | copy-start | bytes 2752516
  1.8 1.5 copy-start.3
  1.9 1.6 copy-start.4
  53.8 4.6 %copy-start.1 = (bf16[1,64,7168]{2,1,0:T(8,128)(2,1)S(1)}, bf16[1,64,7168]{2,1,0:T(8,128)(2,1)}, u32[]{:S(2)}) copy-start(bf16[1,64,7168]{2,1,0:T(8,128)(2,1)} %param.11) | copy-start | bytes 2752516
  53.8 48.7 %all-to-all-start.1 = ((bf16[8,256,896]{1,2,0:T(8,128)(2,1)}), bf16[8,256,896]{1,2,0:T(8,128)(2,1)}, u32[]{:S(2)}, u32[]{:S(2)}) async-start(bf16[8,256,896]{1,2,0:T(8,128)(2,1)} %stack.3), calls=%async_computation.1 | async-start | bytes 7340032 | tf_op jit(solution)/shard_map/all_to_all | solution.py:54
  59.6 49.2 %copy-start.2 = (bf16[1,64,7168]{2,1,0:T(8,128)(2,1)S(1)}, bf16[1,64,7168]{2,1,0:T(8,128)(2,1)}, u32[]{:S(2)}) copy-start(bf16[1,64,7168]{2,1,0:T(8,128)(2,1)} %param.10) | copy-start | bytes 2752516
  102.5 18.0 %all-to-all-start.3 = ((bf16[64,8,896]{2,0,1:T(8,128)(2,1)}), bf16[64,8,896]{2,0,1:T(8,128)(2,1)S(1)}, u32[]{:S(2)}, u32[]{:S(2)}) async-start(bf16[64,8,896]{2,0,1:T(8,128)(2,1)} %copy.35), calls=%async_computation.3 | async-start | bytes 1835008 | tf_op jit(solution)/shard_map/all_to_all | solution.py:59
  133.4 10.8 %copy-start.5 = (f32[16,8]{0,1:T(8,128)S(1)}, f32[16,8]{0,1:T(8,128)}, u32[]{:S(2)}) copy-start(f32[16,8]{0,1:T(8,128)} %param.8) | copy-start | bytes 1540
  137.0 35.2 %all-to-all-start.4 = ((bf16[64,4,896]{2,1,0:T(4,128)(2,1)}), bf16[64,4,896]{2,1,0:T(4,128)(2,1)S(1)}, u32[]{:S(2)}, u32[]{:S(2)}) async-start(bf16[64,4,896]{2,1,0:T(4,128)(2,1)} %reshape.47), calls=%async_computation.4 | async-start | bytes 917504 | tf_op jit(solution)/shard_map/all_to_all | solution.py:71
